TPU v7x, 32 devices: a whole 2x2x4 slice. The times are simulated.
32 devices in a mesh: groups: 2 (over y), inner: 4 (over z), outer: 4 (over x, core).
Axes of the slice: x: 2, y: 2, z: 4, core: 2. Of those that a mesh axis runs over, the one named last changes fastest.
Arguments:
- queries: bfloat16 [8192, 1024], P(('groups', 'outer', 'inner')), parts along dimension 0, may hold values from -6 to 6
- keys: bfloat16 [8192, 1024], P(('groups', 'outer', 'inner')), parts along dimension 0, may hold values from -6 to 6
- values: bfloat16 [8192, 1024], P(('groups', 'outer', 'inner')), parts along dimension 0, may hold values from -6 to 6
- retain: float32 [8192, 8], P(('groups', 'outer', 'inner')), parts along dimension 0, may hold values from 0.4 to 1
- step: float32 [8192, 8], P(('groups', 'outer', 'inner')), parts along dimension 0, may hold values from 0.000625 to 0.0125
- momentum: float32 [8192, 8], P(('groups', 'outer', 'inner')), parts along dimension 0, may hold values from 0.97 to 0.99
- init_memory: float32 [8, 128, 128], replicated, may hold values from -0.1875 to 0.1875
- init_momentum: float32 [8, 128, 128], replicated, may hold values from -0.1875 to 0.1875
Outputs:
- retrieved: bfloat16 [8192, 1024], P(('groups', 'outer', 'inner')), parts along dimension 0
There are 2 independent parts, one for each index of `groups`. A program takes and returns all parts, laid end to end along the dimension named above; an argument that names none is the same for every part. Nothing has to cross between parts.
All inputs are finite; a program needn't handle non-finite values.
Results may differ from a plain program's by a relative error of at most 0.001.
Values sent between devices are 32-bit elements; how exact they have to be, the bound alone decides.
No kernel may reach another device: no remote copies, remote signals or barrier semaphores. Data moves between devices by JAX's collectives and lax.ppermute only.
A program may use at most 256 MiB of HBM per device.

v0:
```python
import jax
import jax.numpy as jnp
from jax import lax
from jax.sharding import PartitionSpec as P


def carried_in(value, axis, join, neutral):
    count, mine = (lax.axis_size(axis), lax.axis_index(axis))
    pieces = jax.tree.map(lambda part: lax.all_gather(part, axis), value)
    total = jax.tree.map(
        lambda part, zero: jnp.full_like(part, 0) + jnp.asarray(zero, part.dtype), value, neutral
    )

    def turn(position, total):
        longer = join(total, jax.tree.map(lambda part: part[position], pieces))
        return jax.tree.map(lambda new, old: jnp.where(position < mine, new, old), longer, total)

    return lax.fori_loop(0, count - 1, turn, total)


def from_root(block, axis, owner):
    block = jnp.where(lax.axis_index(axis) == owner, block, jnp.zeros_like(block))
    return lax.psum(block, axis)


def unit_rows(source, heads):
    rows = source.astype(jnp.float32).reshape(source.shape[0], heads, -1)
    return rows * lax.rsqrt(jnp.sum(rows * rows, -1, keepdims=True) + 1e-06)


def block_terms(queries, keys, values, retain, step, momentum):
    length = queries.shape[0]
    heads = retain.shape[1]
    precise = lax.Precision.HIGHEST
    query_unit = unit_rows(queries, heads)
    key_unit = unit_rows(keys, heads)
    value_rows = values.astype(jnp.float32).reshape(length, heads, -1)
    key_width = key_unit.shape[2]
    log_retain = jnp.cumsum(jnp.log(retain), 0).T
    log_moment = jnp.cumsum(jnp.log(momentum), 0).T
    position = jnp.arange(length)
    causal = (position[:, None] >= position[None, :])[None]
    retain_decay = jnp.where(
        causal,
        jnp.exp(jnp.where(causal, log_retain[:, :, None] - log_retain[:, None, :], 0.0)),
        0.0,
    )
    momentum_decay = jnp.where(
        causal,
        jnp.exp(jnp.where(causal, log_moment[:, :, None] - log_moment[:, None, :], 0.0)),
        0.0,
    )
    weights = jnp.einsum("htu,hur->htr", retain_decay, momentum_decay, precision=precise)
    carry_scale = jnp.einsum("htu,hu->ht", retain_decay, jnp.exp(log_moment), precision=precise)
    scores = jnp.einsum("thd,rhd->htr", query_unit, key_unit, precision=precise)
    step_rows = step.T
    mixing = scores * weights * step_rows[:, None, :]
    memory_weight = weights[:, -1, :] * step_rows
    moment_weight = jnp.exp(log_moment[:, -1:] - log_moment) * step_rows
    memory_gram = jnp.einsum(
        "rhd,hr,rhe->hde", key_unit, memory_weight, key_unit, precision=precise
    )
    moment_gram = jnp.einsum(
        "rhd,hr,rhe->hde", key_unit, moment_weight, key_unit, precision=precise
    )
    identity = jnp.eye(key_width, dtype=jnp.float32)[None]
    retain_end = jnp.exp(log_retain[:, -1])[:, None, None]
    moment_end = jnp.exp(log_moment[:, -1])[:, None, None]
    carry_end = carry_scale[:, -1][:, None, None]
    upper_rows = jnp.concatenate([retain_end * identity - memory_gram, -moment_gram], axis=2)
    lower_rows = jnp.concatenate([carry_end * identity, moment_end * identity], axis=2)
    transition = jnp.concatenate([upper_rows, lower_rows], axis=1)
    memory_write = jnp.einsum(
        "rhd,hr,rhe->hde", value_rows, memory_weight, key_unit, precision=precise
    )
    moment_write = jnp.einsum(
        "rhd,hr,rhe->hde", value_rows, moment_weight, key_unit, precision=precise
    )
    offset = jnp.concatenate([memory_write, moment_write], axis=2)
    local_terms = (query_unit, key_unit, value_rows, jnp.exp(log_retain), carry_scale, mixing)
    return (transition, offset, local_terms)


def block_output(carried, local_terms):
    query_unit, key_unit, value_rows, retain_scale, carry_scale, mixing = local_terms
    precise = lax.Precision.HIGHEST
    key_width = query_unit.shape[2]
    memory = carried[:, :, :key_width]
    moment_part = carried[:, :, key_width:]
    residual = jnp.einsum("rhd,hed->hre", key_unit, memory, precision=precise) - jnp.transpose(
        value_rows, (1, 0, 2)
    )
    result = retain_scale[:, :, None] * jnp.einsum(
        "thd,hed->hte", query_unit, memory, precision=precise
    )
    result = result + carry_scale[:, :, None] * jnp.einsum(
        "thd,hed->hte", query_unit, moment_part, precision=precise
    )
    result = result - jnp.einsum("htr,hre->hte", mixing, residual, precision=precise)
    return jnp.transpose(result, (1, 0, 2)).reshape(query_unit.shape[0], -1).astype(jnp.bfloat16)


def advance_state(carried, transition, offset):
    return jnp.einsum("hij,hjk->hik", carried, transition, precision=lax.Precision.HIGHEST) + offset


def compose(earlier, later):
    joined = jnp.einsum("hij,hjk->hik", earlier[0], later[0], precision=lax.Precision.HIGHEST)
    return (joined, advance_state(earlier[1], later[0], later[1]))


def apply_earlier(gathered, first_state):
    my_group = lax.axis_index("outer")

    def advance_group(index, carried):
        moved = advance_state(carried, gathered[0][index], gathered[1][index])
        return jnp.where(index < my_group, moved, carried)

    return lax.fori_loop(0, gathered[0].shape[0], advance_group, first_state)


def local(queries, keys, values, retain, step, momentum, init_memory, init_momentum):
    transition, offset, local_terms = block_terms(queries, keys, values, retain, step, momentum)
    identity_maps = (
        jnp.broadcast_to(jnp.eye(transition.shape[1], dtype=jnp.float32), transition.shape),
        jnp.zeros_like(offset),
    )
    before = carried_in((transition, offset), "inner", compose, identity_maps)
    through = compose(before, (transition, offset))
    first_state = jnp.concatenate([init_memory, init_momentum], axis=2)
    last_inner = lax.axis_size("inner") - 1
    group_map = (
        from_root(through[0], "inner", last_inner),
        from_root(through[1], "inner", last_inner),
    )
    gathered = (
        lax.all_gather(group_map[0][None], "outer", axis=0, tiled=True),
        lax.all_gather(group_map[1][None], "outer", axis=0, tiled=True),
    )
    entry_state = apply_earlier(gathered, first_state)
    block_state = advance_state(entry_state, before[0], before[1])
    return block_output(block_state, local_terms)


def solution(mesh):
    placed = (
        P(("groups", "outer", "inner"), None),
        P(("groups", "outer", "inner"), None),
        P(("groups", "outer", "inner"), None),
        P(("groups", "outer", "inner"), None),
        P(("groups", "outer", "inner"), None),
        P(("groups", "outer", "inner"), None),
        P(),
        P(),
    )
    return jax.shard_map(
        local,
        mesh=mesh,
        in_specs=placed,
        out_specs=P(("groups", "outer", "inner"), None),
        check_vma=False,
    )
```

profile of v0, /device:TPU:0, one launch (start us, length us, event | category | flops | bytes accessed | tf_op | source)
XLA Modules:
  0.0 601.0 jit_solution(4477719836671399538)
XLA Ops:
  10.5 2.9 fusion.39
  16.8 1.5 copy.116
  18.3 2.1 broadcast_multiply_fusion.1
  21.2 1.6 copy.115
  22.7 2.0 copy.120
  24.8 1.7 convolution_bitcast_fusion.2
  29.2 2.6 copy.125
  32.2 2.3 fusion.44
  35.1 1.4 convolution_negate_fusion
  36.5 1.4 convolution_subtract_fusion.1
  38.9 1.8 copy.119
  41.4 74.1 %all-gather.13.cloned.1.call-done = f32[32,128,256]{2,1,0:T(8,128)} async-done(((f32[8,128,256]{2,1,0:T(8,128)}), f32[32,128,256]{2,1,0:T(8,128)}) %all-gather.13.cloned.1.call-update) | async-done | bytes 4194320 | tf_op jit(solution)/shard_map/all_gather | solution.py:9
  115.4 149.8 %all-gather.11.cloned.1.call-done = f32[32,256,256]{2,1,0:T(8,128)} async-done(((f32[8,256,256]{2,1,0:T(8,128)}), f32[32,256,256]{2,1,0:T(8,128)}) %all-gather.11.cloned.1.call-update) | async-done | bytes 8388624 | tf_op jit(solution)/shard_map/all_gather | solution.py:9
  265.4 49.7 %while.30 = (s32[]{:T(128)}, f32[8,256,256]{1,2,0:T(8,128)S(1)}, f32[8,128,256]{1,2,0:T(8,128)}, s32[]{:T(128)}, f32[4,8,256,256]{3,2,1,0:T(8,128)}, /*index=5*/f32[4,8,128,256]{3,2,1,0:T(8,128)}, s32[]{:T(128)}, s32[]{:T(128)}) while((s32[]{:T(128)}, f32[8,256,256]{1,2,0:T(8,128)S(1)}, f32[8,128,256]{1,2,0:T(8,128)}, s32[]{:T(128)}, ...), condition=%wide.region_7.8_spmd.clone, body=%wide.region_6.7_spmd.clone.sunk | while | flops 2417491968 | bytes 25168492 | solution.py:18
  265.4 2.3 constant_dynamic-slice_fusion.5
  267.7 1.5 copy.193
  270.5 6.1 %fusion.112 = f32[8,128,256]{1,2,0:T(8,128)} fusion(f32[4,8,256,256]{3,2,1,0:T(8,128)} %get-tuple-element.387, s32[]{:T(128)} %get-tuple-element.375, f32[1,8,128,256]{2,3,1,0:T(8,128)S(1)} %copy.193, f32[8,128,256]{1,2,0:T(8,128)S(1)} %copy.218, pred[]{:T(512)S(6)} %compare.3, pred[]{:T(512)S(6)} %lt.44), kind=kOutput, calls=%fused_computation.17.clone.1 | convolution fusion | flops 806354944 | bytes 6293504 | tf_op jit(solution)/shard_map/while/body/eval_jaxpr/hij,hjk->hik/dot_general | solution.py:104
  276.8 5.1 bitcast_select_fusion.2
  281.9 2.3 constant_dynamic-slice_fusion.5
  284.2 1.5 copy.193
  287.0 6.1 %fusion.112 = f32[8,128,256]{1,2,0:T(8,128)} fusion(f32[4,8,256,256]{3,2,1,0:T(8,128)} %get-tuple-element.387, s32[]{:T(128)} %get-tuple-element.375, f32[1,8,128,256]{2,3,1,0:T(8,128)S(1)} %copy.193, f32[8,128,256]{1,2,0:T(8,128)S(1)} %copy.218, pred[]{:T(512)S(6)} %compare.3, pred[]{:T(512)S(6)} %lt.44), kind=kOutput, calls=%fused_computation.17.clone.1 | convolution fusion | flops 806354944 | bytes 6293504 | tf_op jit(solution)/shard_map/while/body/eval_jaxpr/hij,hjk->hik/dot_general | solution.py:104
  293.3 5.1 bitcast_select_fusion.2
  298.4 2.3 constant_dynamic-slice_fusion.5
  300.7 1.5 copy.193
  303.5 6.1 %fusion.112 = f32[8,128,256]{1,2,0:T(8,128)} fusion(f32[4,8,256,256]{3,2,1,0:T(8,128)} %get-tuple-element.387, s32[]{:T(128)} %get-tuple-element.375, f32[1,8,128,256]{2,3,1,0:T(8,128)S(1)} %copy.193, f32[8,128,256]{1,2,0:T(8,128)S(1)} %copy.218, pred[]{:T(512)S(6)} %compare.3, pred[]{:T(512)S(6)} %lt.44), kind=kOutput, calls=%fused_computation.17.clone.1 | convolution fusion | flops 806354944 | bytes 6293504 | tf_op jit(solution)/shard_map/while/body/eval_jaxpr/hij,hjk->hik/dot_general | solution.py:104
  309.8 5.1 bitcast_select_fusion.2
  315.1 5.2 fusion.49
  320.3 4.8 select_bitcast_fusion
  325.2 119.8 %all-reduce.3.cloned.1.call-done = (f32[1,8,256,256]{3,2,1,0:T(8,128)}, f32[1,8,128,256]{2,3,1,0:T(8,128)}) async-done(((f32[1,8,256,256]{3,2,1,0:T(8,128)}, f32[1,8,128,256]{2,3,1,0:T(8,128)}), (f32[1,8,256,256]{3,2,1,0:T(8,128)}, f32[1,8,128,256]{2,3,1,0:T(8,128)})) %all-reduce.3.cloned.1.call-update) | async-done | bytes 3145744 | tf_op jit(solution)/shard_map/psum | solution.py:23
  445.0 2.5 copy.133
  452.1 5.1 fusion.66
  457.2 1.3 copy.138
  458.5 22.6 %all-gather.9.cloned.1.call-done = f32[4,8,128,256]{3,2,1,0:T(8,128)} async-done(((f32[1,8,128,256]{3,2,1,0:T(8,128)}), f32[4,8,128,256]{3,2,1,0:T(8,128)}) %all-gather.9.cloned.1.call-update) | async-done | bytes 4194320 | tf_op jit(solution)/shard_map/all_gather | solution.py:138
  481.2 59.7 %all-gather.7.cloned.1.call-done = f32[4,8,256,256]{3,2,1,0:T(8,128)} async-done(((f32[1,8,256,256]{3,2,1,0:T(8,128)}), f32[4,8,256,256]{3,2,1,0:T(8,128)}) %all-gather.7.cloned.1.call-update) | async-done | bytes 8388624 | tf_op jit(solution)/shard_map/all_gather | solution.py:137
  540.9 41.4 %while.29 = (s32[]{:T(128)}, f32[8,128,256]{1,2,0:T(8,128)}, s32[]{:T(128)}, f32[4,8,256,256]{3,2,1,0:T(8,128)}, f32[4,8,128,256]{3,2,1,0:T(8,128)}, /*index=5*/s32[]{:T(128)}) while((s32[]{:T(128)}, f32[8,128,256]{1,2,0:T(8,128)}, s32[]{:T(128)}, f32[4,8,256,256]{3,2,1,0:T(8,128)}, f32[4,8,128,256]{3,2,1,0:T(8,128)}, ...), condition=%wide.region_11.12_spmd, body=%wide.region_10.11_spmd.sunk | while | flops 805830656 | bytes 16777840 | solution.py:119
  541.1 1.3 constant_dynamic-slice_fusion.4
  542.4 1.3 copy.192
  545.3 6.1 %fusion.107 = f32[8,128,256]{1,2,0:T(8,128)} fusion(f32[8,128,256]{1,2,0:T(8,128)S(1)} %copy.216, f32[4,8,256,256]{3,2,1,0:T(8,128)} %get-tuple-element.406, s32[]{:T(128)} %get-tuple-element.397, f32[1,8,128,256]{2,3,1,0:T(8,128)S(1)} %copy-done, pred[]{:T(512)S(6)} %lt.43), kind=kOutput, calls=%fused_computation.5.clone.1 | convolution fusion | flops 805830656 | bytes 6291969 | tf_op jit(solution)/shard_map/while/body/eval_jaxpr/hij,hjk->hik/dot_general | solution.py:104
  551.4 1.3 constant_dynamic-slice_fusion.4
  552.7 1.3 copy.192
  555.6 6.1 %fusion.107 = f32[8,128,256]{1,2,0:T(8,128)} fusion(f32[8,128,256]{1,2,0:T(8,128)S(1)} %copy.216, f32[4,8,256,256]{3,2,1,0:T(8,128)} %get-tuple-element.406, s32[]{:T(128)} %get-tuple-element.397, f32[1,8,128,256]{2,3,1,0:T(8,128)S(1)} %copy-done, pred[]{:T(512)S(6)} %lt.43), kind=kOutput, calls=%fused_computation.5.clone.1 | convolution fusion | flops 805830656 | bytes 6291969 | tf_op jit(solution)/shard_map/while/body/eval_jaxpr/hij,hjk->hik/dot_general | solution.py:104
  563.0 1.3 copy.192
  565.9 6.1 %fusion.107 = f32[8,128,256]{1,2,0:T(8,128)} fusion(f32[8,128,256]{1,2,0:T(8,128)S(1)} %copy.216, f32[4,8,256,256]{3,2,1,0:T(8,128)} %get-tuple-element.406, s32[]{:T(128)} %get-tuple-element.397, f32[1,8,128,256]{2,3,1,0:T(8,128)S(1)} %copy-done, pred[]{:T(512)S(6)} %lt.43), kind=kOutput, calls=%fused_computation.5.clone.1 | convolution fusion | flops 805830656 | bytes 6291969 | tf_op jit(solution)/shard_map/while/body/eval_jaxpr/hij,hjk->hik/dot_general | solution.py:104
  572.0 1.3 constant_dynamic-slice_fusion.4
  573.3 1.3 copy.192
  576.2 6.1 %fusion.107 = f32[8,128,256]{1,2,0:T(8,128)} fusion(f32[8,128,256]{1,2,0:T(8,128)S(1)} %copy.216, f32[4,8,256,256]{3,2,1,0:T(8,128)} %get-tuple-element.406, s32[]{:T(128)} %get-tuple-element.397, f32[1,8,128,256]{2,3,1,0:T(8,128)S(1)} %copy-done, pred[]{:T(512)S(6)} %lt.43), kind=kOutput, calls=%fused_computation.5.clone.1 | convolution fusion | flops 805830656 | bytes 6291969 | tf_op jit(solution)/shard_map/while/body/eval_jaxpr/hij,hjk->hik/dot_general | solution.py:104
  582.3 4.0 convolution_add_fusion
  589.4 2.5 fusion.45
  (141 shorter events, 34.6 us)
Async XLA Ops:
  6.5 108.9 %all-gather.13.cloned.1.call-start = ((), (), s32[]{:S(2)}) async-start(), calls=%async_computation.3 | async-start | bytes 5242880 | tf_op jit(solution)/shard_map/all_gather | solution.py:9
  6.6 6.9 %copy-start.25 = (pred[256,256]{1,0:T(8,128)(4,1)}, pred[256,256]{1,0:T(8,128)(4,1)S(1)}, u32[]{:S(2)}) copy-start(pred[256,256]{1,0:T(8,128)(4,1)S(1)} %iota_compare_fusion) | copy-start | bytes 196612
  8.2 5.3 copy-start.28
  10.5 3.0 copy-start.31
  10.5 3.0 copy-start.27
  10.5 4.4 copy-start.21
  13.5 1.3 copy-start.16
  15.1 1.0 copy-start.22
  18.3 2.1 copy-start.23
  20.4 16.1 %copy-start.2 = (f32[256,8,128]{2,1,0:T(8,128)}, f32[256,8,128]{2,1,0:T(8,128)S(1)}, u32[]{:S(2)}) copy-start(f32[256,8,128]{2,1,0:T(8,128)S(1)} %get-tuple-element.291) | copy-start | bytes 3145732
  24.8 1.7 copy-start.6
  26.5 0.8 copy-start.19
  27.3 0.8 copy-start.20
  29.2 3.0 copy-start.32
  29.2 3.0 copy-start.26
  29.2 3.0 copy-start.29
  29.2 3.0 copy-start.30
  31.8 233.4 %all-gather.11.cloned.1.call-start = ((), (), s32[]{:S(2)}) async-start(), calls=%async_computation.2 | async-start | bytes 10485760 | tf_op jit(solution)/shard_map/all_gather | solution.py:9
  35.1 2.9 copy-start.8
  35.1 2.9 copy-start.10
  36.5 1.5 copy-start.12
  38.0 0.8 copy-start.14
  40.7 404.2 %all-reduce.3.cloned.1.call-start = ((), (), s32[]{:S(2)}) async-start(), calls=%async_computation.4 | async-start | bytes 6291456 | tf_op jit(solution)/shard_map/psum | solution.py:23
  315.1 5.2 copy-start.9
  315.1 5.2 copy-start.11
  315.1 5.2 copy-start.13
  315.1 5.2 copy-start.15
  325.2 156.0 %all-gather.9.cloned.1.call-start = ((), (), s32[]{:S(2)}) async-start(), calls=%async_computation.1 | async-start | bytes 5242880 | tf_op jit(solution)/shard_map/all_gather | solution.py:138
  447.5 1.0 copy-start.7
  447.5 2.0 copy-start.24
  447.5 93.4 %all-gather.7.cloned.1.call-start = ((), (), s32[]{:S(2)}) async-start(), calls=%async_computation | async-start | bytes 10485760 | tf_op jit(solution)/shard_map/all_gather | solution.py:137
  452.1 5.1 copy-start.1
  543.8 1.5 copy-start
  554.1 1.5 copy-start
  564.4 1.5 copy-start
  574.7 1.5 copy-start
  582.3 4.0 copy-start.4
  586.3 1.3 copy-start.3
  586.3 1.3 copy-start.18
  586.3 2.5 copy-start.17
  587.6 1.7 copy-start.5
Sparse Core Ops, SparseCore 0:
  31.9 83.4 all-gather.12
  117.0 148.1 all-gather.10
  325.3 119.6 all-reduce.2
  447.7 33.4 all-gather.8
  482.6 58.2 all-gather.6
where the time goes:
time: 609 us; the launch traced here: 601 us
  waiting for transfers between devices  427 us (70%)
  matrix products  93.8 us (15%)
  local copies, waits for them, and re-layouts  56.5 us (9%)
  between operations  13.9 us (2%)
  other arithmetic  8.6 us (1%)
    all_gather x2, waiting for transfers between devices, carried_in(): pieces = jax.tree.map(lambda part: lax.all_gather(part, axis), value)  224 us
    psum x1, waiting for transfers between devices, from_root(): return lax.psum(block, axis)  120 us
    all_gather x1, waiting for transfers between devices, local(): lax.all_gather(group_map[0][None], 'outer', axis=0, tiled=True)  59.7 us
    dot_general x9, matrix products, advance_state(): jnp.einsum('hij,hjk->hik', carried, transition, precision=lax.Precision.H...  51.8 us
    all_gather x1, waiting for transfers between devices, local(): lax.all_gather(group_map[1][None], 'outer', axis=0, tiled=True)  22.6 us
    dot_general x4, matrix products, compose(): jnp.einsum('hij,hjk->hik', earlier[0], later[0], precision=lax.Precision....  20.2 us
  transfers between devices with their start and end apart: 5, of which 5 were waited for; matrix products, arithmetic and copies ran while one was open for 3% of the time, Pallas kernels for 0%

commit v1 on v0

--- a/solution.py
+++ b/solution.py
@@ -2,6 +2,17 @@
 import jax.numpy as jnp
 from jax import lax
 from jax.sharding import PartitionSpec as P
+
+
+def ring_gather(x, axis, dim):
+    ways = lax.axis_size(axis)
+    pieces = [x]
+    for far in range(1, ways):
+        pieces.append(
+            lax.ppermute(pieces[far - 1], axis, [(d, (d - 1) % ways) for d in range(ways)])
+        )
+    line = jnp.concatenate(pieces, axis=dim)
+    return jnp.roll(line, lax.axis_index(axis) * x.shape[dim], axis=dim)
 
 
 def carried_in(value, axis, join, neutral):
@@ -135,7 +146,7 @@
     )
     gathered = (
         lax.all_gather(group_map[0][None], "outer", axis=0, tiled=True),
-        lax.all_gather(group_map[1][None], "outer", axis=0, tiled=True),
+        ring_gather(group_map[1][None], "outer", 0),
     )
     entry_state = apply_earlier(gathered, first_state)
     block_state = advance_state(entry_state, before[0], before[1])

time: 609 us -> 580 us (0.952)
  waiting for transfers between devices: 427 us -> 402 us
  local copies, waits for them, and re-layouts: 56.5 us -> 50.4 us
    all_gather x1, waiting for transfers between devices: 59.7 us -> 0.01 us  [local(): lax.all_gather(group_map[0][None], 'outer', axis=0, tiled=True)]
    ppermute x0 -> x3, waiting for transfers between devices: none -> 58.8 us  [ring_gather(): lax.ppermute(pieces[far - 1], axis, [(d, (d - 1) % ways) for d in range(w...]
    all_gather x1 -> x0, waiting for transfers between devices: 22.6 us -> none  [local(): lax.all_gather(group_map[1][None], 'outer', axis=0, tiled=True)]
    unnamed x69 -> x80, local copies, waits for them, and re-layouts: 7.74 us -> 16.5 us
    dynamic_slice x8 -> x1, local copies, waits for them, and re-layouts: 10.7 us -> 2.31 us  [ring_gather(): return jnp.roll(line, lax.axis_index(axis) * x.shape[dim], axis=dim)]
  transfers between devices with their start and end apart: 5 -> 7, of which waited for: 5 -> 6; matrix products, arithmetic and copies ran while one was open for 3% -> 5% of each run, Pallas kernels for 0% -> 0%
where the time goes in v1:
time: 580 us; the launch traced here: 573 us
  waiting for transfers between devices  402 us (69%)
  matrix products  90.7 us (16%)
  local copies, waits for them, and re-layouts  50.4 us (9%)
  between operations  14 us (2%)
  other arithmetic  8.09 us (1%)
  starting transfers between devices  6.37 us (1%)
    all_gather x2, waiting for transfers between devices, carried_in(): pieces = jax.tree.map(lambda part: lax.all_gather(part, axis), value)  224 us
    psum x1, waiting for transfers between devices, from_root(): return lax.psum(block, axis)  120 us
    ppermute x3, waiting for transfers between devices, ring_gather(): lax.ppermute(pieces[far - 1], axis, [(d, (d - 1) % ways) for d in range(w...  58.8 us
    dot_general x9, matrix products, advance_state(): jnp.einsum('hij,hjk->hik', carried, transition, precision=lax.Precision.H...  48.9 us
    dot_general x4, matrix products, compose(): jnp.einsum('hij,hjk->hik', earlier[0], later[0], precision=lax.Precision....  20.2 us
    unnamed x80, local copies, waits for them, and re-layouts  16.5 us
    dynamic_slice x6, local copies, waits for them, and re-layouts, turn(): longer = join(total, jax.tree.map(lambda part: part[position], pieces))  11.6 us
  transfers between devices with their start and end apart: 7, of which 6 were waited for; matrix products, arithmetic and copies ran while one was open for 5% of the time, Pallas kernels for 0%

profile of v1, /device:TPU:0, one launch (start us, length us, event | category | flops | bytes accessed | tf_op | source)
XLA Modules:
  0.0 572.6 jit_solution(14065272494016560587)
XLA Ops:
  10.5 2.9 fusion.39
  13.5 1.3 copy-done.17
  17.7 2.1 broadcast_multiply_fusion.1
  20.6 1.6 copy.115
  22.2 2.0 copy.120
  24.2 1.7 convolution_bitcast_fusion.2
  28.6 2.6 copy.125
  31.6 2.3 fusion.44
  34.5 1.4 convolution_negate_fusion
  35.9 1.4 convolution_subtract_fusion.1
  38.4 1.8 copy.119
  40.9 74.0 %all-gather.10.cloned.1.call-done = f32[32,128,256]{2,1,0:T(8,128)} async-done(((f32[8,128,256]{2,1,0:T(8,128)}), f32[32,128,256]{2,1,0:T(8,128)}) %all-gather.10.cloned.1.call-update) | async-done | bytes 4194320 | tf_op jit(solution)/shard_map/all_gather | solution.py:20
  114.9 149.8 %all-gather.8.cloned.1.call-done = f32[32,256,256]{2,1,0:T(8,128)} async-done(((f32[8,256,256]{2,1,0:T(8,128)}), f32[32,256,256]{2,1,0:T(8,128)}) %all-gather.8.cloned.1.call-update) | async-done | bytes 8388624 | tf_op jit(solution)/shard_map/all_gather | solution.py:20
  264.8 49.7 %while.30 = (s32[]{:T(128)}, f32[8,256,256]{1,2,0:T(8,128)S(1)}, f32[8,128,256]{1,2,0:T(8,128)}, s32[]{:T(128)}, f32[4,8,256,256]{3,2,1,0:T(8,128)}, /*index=5*/f32[4,8,128,256]{3,2,1,0:T(8,128)}, s32[]{:T(128)}, s32[]{:T(128)}) while((s32[]{:T(128)}, f32[8,256,256]{1,2,0:T(8,128)S(1)}, f32[8,128,256]{1,2,0:T(8,128)}, s32[]{:T(128)}, ...), condition=%wide.region_7.8_spmd.clone, body=%wide.region_6.7_spmd.clone.sunk | while | flops 2417491968 | bytes 25168492 | solution.py:29
  264.8 2.3 constant_dynamic-slice_fusion.3
  267.1 1.5 copy.188
  269.9 6.1 %fusion.112 = f32[8,128,256]{1,2,0:T(8,128)} fusion(f32[4,8,256,256]{3,2,1,0:T(8,128)} %get-tuple-element.387, s32[]{:T(128)} %get-tuple-element.375, f32[1,8,128,256]{2,3,1,0:T(8,128)S(1)} %copy.188, f32[8,128,256]{1,2,0:T(8,128)S(1)} %copy.220, pred[]{:T(512)S(6)} %compare.4, pred[]{:T(512)S(6)} %lt.58), kind=kOutput, calls=%fused_computation.16.clone.1 | convolution fusion | flops 806354944 | bytes 6293504 | tf_op jit(solution)/shard_map/while/body/eval_jaxpr/hij,hjk->hik/dot_general | solution.py:115
  276.2 5.1 bitcast_select_fusion.2
  281.4 2.3 constant_dynamic-slice_fusion.3
  283.7 1.5 copy.188
  286.5 6.1 %fusion.112 = f32[8,128,256]{1,2,0:T(8,128)} fusion(f32[4,8,256,256]{3,2,1,0:T(8,128)} %get-tuple-element.387, s32[]{:T(128)} %get-tuple-element.375, f32[1,8,128,256]{2,3,1,0:T(8,128)S(1)} %copy.188, f32[8,128,256]{1,2,0:T(8,128)S(1)} %copy.220, pred[]{:T(512)S(6)} %compare.4, pred[]{:T(512)S(6)} %lt.58), kind=kOutput, calls=%fused_computation.16.clone.1 | convolution fusion | flops 806354944 | bytes 6293504 | tf_op jit(solution)/shard_map/while/body/eval_jaxpr/hij,hjk->hik/dot_general | solution.py:115
  292.7 5.1 bitcast_select_fusion.2
  297.9 2.3 constant_dynamic-slice_fusion.3
  300.2 1.5 copy.188
  303.0 6.1 %fusion.112 = f32[8,128,256]{1,2,0:T(8,128)} fusion(f32[4,8,256,256]{3,2,1,0:T(8,128)} %get-tuple-element.387, s32[]{:T(128)} %get-tuple-element.375, f32[1,8,128,256]{2,3,1,0:T(8,128)S(1)} %copy.188, f32[8,128,256]{1,2,0:T(8,128)S(1)} %copy.220, pred[]{:T(512)S(6)} %compare.4, pred[]{:T(512)S(6)} %lt.58), kind=kOutput, calls=%fused_computation.16.clone.1 | convolution fusion | flops 806354944 | bytes 6293504 | tf_op jit(solution)/shard_map/while/body/eval_jaxpr/hij,hjk->hik/dot_general | solution.py:115
  309.2 5.1 bitcast_select_fusion.2
  314.6 5.3 fusion.49
  319.9 4.8 select_bitcast_fusion
  324.8 119.7 %all-reduce.3.cloned.1.call-done = (f32[1,8,256,256]{3,2,1,0:T(8,128)}, f32[1,8,128,256]{2,3,1,0:T(8,128)}) async-done(((f32[1,8,256,256]{3,2,1,0:T(8,128)}, f32[1,8,128,256]{2,3,1,0:T(8,128)}), (f32[1,8,256,256]{3,2,1,0:T(8,128)}, f32[1,8,128,256]{2,3,1,0:T(8,128)})) %all-reduce.3.cloned.1.call-update) | async-done | bytes 3145744 | tf_op jit(solution)/shard_map/psum | solution.py:34
  445.5 19.7 %collective-permute-done = f32[1,8,128,256]{2,3,1,0:T(8,128)S(1)} collective-permute-done((f32[1,8,128,256]{2,3,1,0:T(8,128)}, f32[1,8,128,256]{2,3,1,0:T(8,128)S(1)}, u32[]{:S(2)}, u32[]{:S(2)}) %collective-permute-start) | collective-permute-done | bytes 1048608 | tf_op jit(solution)/shard_map/ppermute | solution.py:12
  466.2 2.2 collective-permute-start.1
  468.4 34.8 %collective-permute-done.1 = f32[1,8,128,256]{2,3,1,0:T(8,128)} collective-permute-done((f32[1,8,128,256]{2,3,1,0:T(8,128)S(1)}, f32[1,8,128,256]{2,3,1,0:T(8,128)}, u32[]{:S(2)}, u32[]{:S(2)}) %collective-permute-start.1) | collective-permute-done | bytes 1048608 | tf_op jit(solution)/shard_map/ppermute | solution.py:12
  503.2 2.3 collective-permute-start.2
  507.5 2.1 copy.112
  510.8 4.9 fusion.66
  515.7 2.5 copy.136
  518.2 1.4 constant_dynamic-update-slice_fusion.7
  519.9 1.4 constant_dynamic-update-slice_fusion.5
  521.2 4.3 collective-permute-done.2
  529.6 2.3 constant_dynamic-slice_fusion.1
  531.9 22.2 %while.29 = (s32[]{:T(128)}, f32[8,128,256]{1,2,0:T(8,128)S(1)}, s32[]{:T(128)}, f32[4,8,256,256]{3,2,1,0:T(8,128)}, f32[4,8,128,256]{2,3,1,0:T(8,128)}, /*index=5*/s32[]{:T(128)}) while((s32[]{:T(128)}, f32[8,128,256]{1,2,0:T(8,128)S(1)}, s32[]{:T(128)}, f32[4,8,256,256]{3,2,1,0:T(8,128)}, f32[4,8,128,256]{2,3,1,0:T(8,128)}, ...), condition=%wide.region_11.12_spmd, body=%wide.region_10.11_spmd.sunk | while | flops 805830656 | bytes 8389711 | solution.py:130
  532.2 5.4 fusion.107
  537.7 5.4 fusion.107
  543.2 5.4 fusion.107
  548.7 5.4 fusion.107
  554.2 3.7 convolution_add_fusion
  560.9 2.6 fusion.45
  563.5 1.3 fusion.54
  (140 shorter events, 30.7 us)
Async XLA Ops:
  6.5 108.3 %all-gather.10.cloned.1.call-start = ((), (), s32[]{:S(2)}) async-start(), calls=%async_computation.2 | async-start | bytes 5242880 | tf_op jit(solution)/shard_map/all_gather | solution.py:20
  6.6 6.9 %copy-start.26 = (pred[256,256]{1,0:T(8,128)(4,1)}, pred[256,256]{1,0:T(8,128)(4,1)S(1)}, u32[]{:S(2)}) copy-start(pred[256,256]{1,0:T(8,128)(4,1)S(1)} %iota_compare_fusion) | copy-start | bytes 196612
  8.2 5.3 copy-start.29
  10.5 4.3 copy-start.32
  10.5 4.3 copy-start.28
  10.5 4.5 copy-start.22
  13.5 1.3 copy-start.17
  15.2 1.0 copy-start.23
  17.7 2.1 copy-start.24
  19.9 16.1 %copy-start = (f32[256,8,128]{2,1,0:T(8,128)}, f32[256,8,128]{2,1,0:T(8,128)S(1)}, u32[]{:S(2)}) copy-start(f32[256,8,128]{2,1,0:T(8,128)S(1)} %get-tuple-element.291) | copy-start | bytes 3145732
  24.2 1.7 copy-start.4
  26.0 0.8 copy-start.20
  26.8 0.8 copy-start.21
  28.6 3.0 copy-start.33
  28.6 3.0 copy-start.27
  28.6 3.0 copy-start.30
  28.6 3.0 copy-start.31
  31.2 233.4 %all-gather.8.cloned.1.call-start = ((), (), s32[]{:S(2)}) async-start(), calls=%async_computation.1 | async-start | bytes 10485760 | tf_op jit(solution)/shard_map/all_gather | solution.py:20
  34.5 2.9 copy-start.6
  34.5 2.9 copy-start.8
  35.9 1.5 copy-start.10
  37.4 0.9 copy-start.12
  40.2 404.3 %all-reduce.3.cloned.1.call-start = ((), (), s32[]{:S(2)}) async-start(), calls=%async_computation.3 | async-start | bytes 6291456 | tf_op jit(solution)/shard_map/psum | solution.py:34
  314.6 5.3 copy-start.7
  314.6 5.3 copy-start.9
  314.6 5.3 copy-start.11
  314.6 5.3 copy-start.13
  324.7 180.8 %copy-start.5 = (bf16[256,1024]{0,1:T(8,128)(2,1)S(1)}, bf16[256,1024]{0,1:T(8,128)(2,1)}, u32[]{:S(2)}) copy-start(bf16[256,1024]{0,1:T(8,128)(2,1)} %copy.120) | copy-start | bytes 1572868
  324.7 181.7 %copy-start.25 = (f32[8,128,128]{2,1,0:T(8,128)S(1)}, f32[8,128,128]{2,1,0:T(8,128)}, u32[]{:S(2)}) copy-start(f32[8,128,128]{2,1,0:T(8,128)} %param.18) | copy-start | bytes 1572868
  324.7 207.2 %all-gather.6.cloned.1.call-start = ((), (), s32[]{:S(2)}) async-start(), calls=%async_computation | async-start | bytes 10485760 | tf_op jit(solution)/shard_map/all_gather | solution.py:148
  444.6 20.7 %collective-permute-start = (f32[1,8,128,256]{2,3,1,0:T(8,128)}, f32[1,8,128,256]{2,3,1,0:T(8,128)S(1)}, u32[]{:S(2)}, u32[]{:S(2)}) collective-permute-start(f32[1,8,128,256]{2,3,1,0:T(8,128)} %get-tuple-element.287), channel_id=1, source_target_pairs={{0,3},{1,0},{2,1},{3,2},{4,7},{5,4},{6,5},{7,6},{8,11},{9,8},{10,9... | collective-permute-start | bytes 3145736 | tf_op jit(solution)/shard_map/ppermute | solution.py:12
  465.2 1.0 copy-start.15
  466.2 37.0 %collective-permute-start.1 = (f32[1,8,128,256]{2,3,1,0:T(8,128)S(1)}, f32[1,8,128,256]{2,3,1,0:T(8,128)}, u32[]{:S(2)}, u32[]{:S(2)}) collective-permute-start(f32[1,8,128,256]{2,3,1,0:T(8,128)S(1)} %collective-permute-done), channel_id=1, source_target_pairs={{0,3},{1,0},{2,1},{3,2},{4,7},{5,4},{6,5},{7,6},{8,11},{9,8},{10,9... | collective-permute-start | bytes 3145736 | tf_op jit(solution)/shard_map/ppermute | solution.py:12
  503.2 22.4 %collective-permute-start.2 = (f32[1,8,128,256]{2,3,1,0:T(8,128)}, f32[1,8,128,256]{2,3,1,0:T(8,128)}, u32[]{:S(2)}, u32[]{:S(2)}) collective-permute-start(f32[1,8,128,256]{2,3,1,0:T(8,128)} %collective-permute-done.1), channel_id=1, source_target_pairs={{0,3},{1,0},{2,1},{3,2},{4,7},{5,4},{6,5},{7,6},{8,11},{9,8},{10,9... | collective-permute-start | bytes 3145736 | tf_op jit(solution)/shard_map/ppermute | solution.py:12
  518.2 1.5 copy-start.16
  519.8 7.0 %copy-start.14 = (f32[1,8,128,256]{2,3,1,0:T(8,128)S(1)}, f32[1,8,128,256]{2,3,1,0:T(8,128)}, u32[]{:S(2)}) copy-start(f32[1,8,128,256]{2,3,1,0:T(8,128)} %get-tuple-element.287) | copy-start | bytes 3145732
  554.1 3.7 copy-start.2
  557.8 1.3 copy-start.1
  557.8 1.3 copy-start.19
  557.9 2.5 copy-start.18
  559.2 1.7 copy-start.3
Sparse Core Ops, SparseCore 0:
  31.4 83.4 all-gather.9
  116.4 148.1 all-gather.7
  324.9 119.6 all-reduce.2
  446.0 75.8 all-gather.5
